TPU v7x, 32 devices: a whole 2x2x4 slice. The times are simulated.
32 devices in a mesh: dp: 8 (over z, y), mp: 4 (over x, core).
Axes of the slice: x: 2, y: 2, z: 4, core: 2. Of those that a mesh axis runs over, the one named last changes fastest.
Arguments:
- tokens: bfloat16 [2, 16384, 768], P(None, ('dp', 'mp')), may hold values from -6 to 6
- cotangent: bfloat16 [2, 16384, 768], P(None, ('dp', 'mp')), may hold values from -6 to 6
- lengths: int32 [2, 16], P(None, 'dp'), may hold values from 341 to 1024, as said below
- w_query: bfloat16 [768, 768], P('dp', 'mp'), may hold values from -0.3125 to 0.3125
- w_key: bfloat16 [768, 768], P('dp', 'mp'), may hold values from -0.21875 to 0.21875
- w_value: bfloat16 [768, 768], P('dp', 'mp'), may hold values from -0.21875 to 0.21875
- w_out: bfloat16 [768, 768], P(('mp', 'dp')), may hold values from -0.875 to 0.875
- w_up: bfloat16 [768, 3072], P('dp', 'mp'), may hold values from -0.21875 to 0.21875
- w_down: bfloat16 [3072, 768], P(('mp', 'dp')), may hold values from -0.109375 to 0.109375
- b_query: float32 [768], P('mp'), may hold values from -3 to 3
- b_value: float32 [768], P('mp'), may hold values from -0.6 to 0.6
- b_up: float32 [3072], P('mp'), may hold values from -3 to 3
- b_out: float32 [768], replicated, may hold values from -0.6 to 0.6
- b_down: float32 [768], replicated, may hold values from -1.2 to 1.2
- norm1_gain: float32 [768], replicated, may hold values from 0.25 to 1.75
- norm1_shift: float32 [768], replicated, may hold values from -1.2 to 1.2
- norm2_gain: float32 [768], replicated, may hold values from 0.25 to 1.75
- norm2_shift: float32 [768], replicated, may hold values from -1.2 to 1.2
Outputs:
- output: bfloat16 [2, 16384, 768], P(None, ('dp', 'mp'))
- tokens_grad: float32 [2, 16384, 768], P(None, ('dp', 'mp'))
- w_query_grad: float32 [768, 768], P('dp', 'mp')
- w_key_grad: float32 [768, 768], P('dp', 'mp')
- w_value_grad: float32 [768, 768], P('dp', 'mp')
- w_out_grad: float32 [768, 768], P(('mp', 'dp'))
- w_up_grad: float32 [768, 3072], P('dp', 'mp')
- w_down_grad: float32 [3072, 768], P(('mp', 'dp'))
- b_query_grad: float32 [768], P(('mp', 'dp'))
- b_value_grad: float32 [768], P(('mp', 'dp'))
- b_up_grad: float32 [3072], P(('mp', 'dp'))
- b_out_grad: float32 [768], P(('dp', 'mp'))
- b_down_grad: float32 [768], P(('dp', 'mp'))
- norm1_gain_grad: float32 [768], P(('dp', 'mp'))
- norm1_shift_grad: float32 [768], P(('dp', 'mp'))
- norm2_gain_grad: float32 [768], P(('dp', 'mp'))
- norm2_shift_grad: float32 [768], P(('dp', 'mp'))
- rms_values: float32 [3], replicated
Inputs may be any that keep to these rules, and one draw needn't show every extreme that they name: The last sequence of every micro-batch has all 1024 positions valid; lengths tend to grow with the sequence's index.
All inputs are finite; a program needn't handle non-finite values.
Results may differ from a plain program's by a relative error of at most 0.019.
Values may be sent and summed in bfloat16 or wider, within the bound.
A program may use at most 192 MiB of HBM per device.

v0:
```python
import jax
import jax.numpy as jnp
from jax import lax
from jax.sharding import PartitionSpec as P

HD = 64
L = 1024
SEQ_MB = 2
MB = 2


epsilon = 1e-05
masked_score = -1e30


def cut_along(shard, dim, size):
    shape = shard.shape
    tiles = shard.reshape(*shape[:dim], size, shape[dim] // size, *shape[dim + 1 :])
    return jnp.moveaxis(tiles, dim, 0)


def summed_on_arrival(shard, axis, dim):
    size = lax.axis_size(axis)
    tiles = lax.all_to_all(cut_along(shard, dim, size), axis, 0, 0, tiled=True)
    return jnp.sum(tiles.astype(jnp.float32), axis=0)


def in_one_piece(arrays, axis, dim, along):
    ends, at = ([], 0)
    for a in arrays[:-1]:
        at += a.shape[along]
        ends.append(at)
    both = jnp.concatenate(arrays, axis=along)
    return tuple(jnp.split(summed_on_arrival(both, axis, dim), ends, axis=along))


def product(left_side, right_side):
    return jnp.dot(left_side, right_side, preferred_element_type=jnp.float32)


def contract_rows(left_side, right_side):
    return lax.dot_general(
        left_side, right_side, (((0,), (0,)), ((), ())), preferred_element_type=jnp.float32
    )


def contract_cols(left_side, right_side):
    return lax.dot_general(
        left_side, right_side, (((1,), (1,)), ((), ())), preferred_element_type=jnp.float32
    )


def layer_norm(values, norm_gain, norm_shift):
    center = values - jnp.mean(values, axis=-1, keepdims=True)
    spread = jnp.mean(center * center, axis=-1, keepdims=True)
    inverse = lax.rsqrt(spread + epsilon)
    scaled = center * inverse
    return (scaled * norm_gain + norm_shift, scaled, inverse)


def norm_back(upstream, scaled, inverse, norm_gain):
    gain_grad = jnp.sum(upstream * scaled, axis=0)
    shift_grad = jnp.sum(upstream, axis=0)
    through = upstream * norm_gain
    result = inverse * (
        through
        - jnp.mean(through, axis=-1, keepdims=True)
        - scaled * jnp.mean(through * scaled, axis=-1, keepdims=True)
    )
    return (result, gain_grad, shift_grad)


def gelu_slope(preact):
    cumulative = 0.5 * (1.0 + jax.scipy.special.erf(preact * 0.7071067811865476))
    density = jnp.exp(-0.5 * preact * preact) * 0.3989422804014327
    return cumulative + preact * density


def attend_forward(queries, keys_all, values_all, length, block_rows, score_scale):
    seq_len = keys_all.shape[0]
    visible = (jnp.arange(seq_len) < length)[None, None, :]

    def one_block(start_row):
        query_block = lax.dynamic_slice_in_dim(queries, start_row, block_rows, 0)
        scores = (
            jnp.einsum("qhd,khd->hqk", query_block, keys_all, preferred_element_type=jnp.float32)
            * score_scale
        )
        scores = jnp.where(visible, scores, masked_score)
        highest = jnp.max(scores, axis=-1, keepdims=True)
        exp_scores = jnp.exp(scores - highest)
        exp_total = jnp.sum(exp_scores, axis=-1, keepdims=True)
        attn_probs = (exp_scores / exp_total).astype(jnp.bfloat16)
        heads_out = jnp.einsum(
            "hqk,khd->qhd", attn_probs, values_all, preferred_element_type=jnp.float32
        )
        return (heads_out, highest[..., 0] + jnp.log(exp_total[..., 0]))

    starts = jnp.arange(seq_len // block_rows, dtype=jnp.int32) * block_rows
    heads_out, logsum = lax.map(one_block, starts)
    return (heads_out.reshape(queries.shape), logsum)


def attend_backward(
    queries, keys_all, values_all, length, logsum, heads_grad, block_rows, score_scale
):
    seq_len = keys_all.shape[0]
    visible = (jnp.arange(seq_len) < length)[None, None, :]

    def one_block(state_now, block_data):
        key_grad, value_grad = state_now
        start_row, block_logsum = block_data
        query_block = lax.dynamic_slice_in_dim(queries, start_row, block_rows, 0)
        grad_block = lax.dynamic_slice_in_dim(heads_grad, start_row, block_rows, 0)
        scores = (
            jnp.einsum("qhd,khd->hqk", query_block, keys_all, preferred_element_type=jnp.float32)
            * score_scale
        )
        scores = jnp.where(visible, scores, masked_score)
        attn_probs = jnp.exp(scores - block_logsum[..., None])
        probs_low = attn_probs.astype(jnp.bfloat16)
        prob_grad = jnp.einsum(
            "qhd,khd->hqk", grad_block, values_all, preferred_element_type=jnp.float32
        )
        row_dot = jnp.sum(prob_grad * attn_probs, axis=-1, keepdims=True)
        score_grad = (attn_probs * (prob_grad - row_dot)).astype(jnp.bfloat16)
        query_grad = (
            jnp.einsum("hqk,khd->qhd", score_grad, keys_all, preferred_element_type=jnp.float32)
            * score_scale
        )
        key_grad = (
            key_grad
            + jnp.einsum(
                "hqk,qhd->khd", score_grad, query_block, preferred_element_type=jnp.float32
            )
            * score_scale
        )
        value_grad = value_grad + jnp.einsum(
            "hqk,qhd->khd", probs_low, grad_block, preferred_element_type=jnp.float32
        )
        return ((key_grad, value_grad), query_grad)

    starts = jnp.arange(seq_len // block_rows, dtype=jnp.int32) * block_rows
    zero_grads = jnp.zeros(keys_all.shape, jnp.float32)
    (key_grad, value_grad), query_grad = lax.scan(
        one_block, (zero_grads, zero_grads), (starts, logsum)
    )
    return (query_grad.reshape(queries.shape), key_grad, value_grad)


def body(
    tokens,
    cotangent,
    lengths,
    w_query,
    w_key,
    w_value,
    w_out,
    w_up,
    w_down,
    b_query,
    b_value,
    b_up,
    b_out,
    b_down,
    norm1_gain,
    norm1_shift,
    norm2_gain,
    norm2_shift,
):
    shard_rows = tokens.shape[1]
    model_width = tokens.shape[2]
    row_count = shard_rows * lax.axis_size("mp")
    head_cols = w_query.shape[1]
    head_count = head_cols // HD
    unit_cols = w_up.shape[1]
    block_rows = min(512, L)
    score_scale = HD ** (-0.5)
    four_shape = (SEQ_MB, L, head_count, HD)
    mp_index = lax.axis_index("mp")
    weight_shard = (w_query, w_key, w_value, w_out, w_up, w_down)
    joined_bias = jnp.concatenate([b_query, jnp.zeros_like(b_query), b_value])
    positions = mp_index * shard_rows + jnp.arange(shard_rows, dtype=jnp.int32)
    owners = positions // L
    places = positions % L
    seq_ids = jnp.arange(SEQ_MB, dtype=jnp.int32)
    joined_wgrad = jnp.zeros((model_width, 3 * head_cols), jnp.float32)
    out_wgrad = jnp.zeros((head_cols, model_width), jnp.float32)
    up_wgrad = jnp.zeros((model_width, unit_cols), jnp.float32)
    down_wgrad = jnp.zeros((unit_cols, model_width), jnp.float32)
    query_bias_grad = jnp.zeros((head_cols,), jnp.float32)
    value_bias_grad = jnp.zeros((head_cols,), jnp.float32)
    up_bias_grad = jnp.zeros((unit_cols,), jnp.float32)
    out_bias_grad = jnp.zeros((model_width,), jnp.float32)
    down_bias_grad = jnp.zeros((model_width,), jnp.float32)
    gain1_grad = jnp.zeros((model_width,), jnp.float32)
    shift1_grad = jnp.zeros((model_width,), jnp.float32)
    gain2_grad = jnp.zeros((model_width,), jnp.float32)
    shift2_grad = jnp.zeros((model_width,), jnp.float32)
    squares = [jnp.zeros((), jnp.float32) for index_unused in range(4)]
    outputs = []
    input_grads = []
    for micro_idx in range(MB):
        forward_weights = (
            lax.all_gather(weight_shard[0], "dp", axis=0, tiled=True),
            lax.all_gather(weight_shard[1], "dp", axis=0, tiled=True),
            lax.all_gather(weight_shard[2], "dp", axis=0, tiled=True),
            lax.all_gather(weight_shard[3], "dp", axis=0, tiled=True),
            lax.all_gather(weight_shard[4], "dp", axis=0, tiled=True),
            lax.all_gather(weight_shard[5], "dp", axis=0, tiled=True),
        )
        full_query, full_key, full_value, full_out, full_up, full_down = forward_weights
        joined = jnp.concatenate([full_query, full_key, full_value], axis=1)
        seq_lengths = lengths[micro_idx]
        own_rows = tokens[micro_idx]
        gathered_rows = lax.all_gather(own_rows, "mp", axis=0, tiled=True)
        projected = (product(gathered_rows, joined) + joined_bias).astype(jnp.bfloat16)
        queries = projected[:, :head_cols].reshape(four_shape)
        keys_all = projected[:, head_cols : 2 * head_cols].reshape(four_shape)
        values_all = projected[:, 2 * head_cols :].reshape(four_shape)

        def forward_seq(packed):
            return attend_forward(
                packed[0], packed[1], packed[2], packed[3], block_rows, score_scale
            )

        heads_out, logsum = lax.map(forward_seq, (queries, keys_all, values_all, seq_lengths))
        heads_low = heads_out.reshape(row_count, head_cols).astype(jnp.bfloat16)
        attention = (
            lax.psum_scatter(
                product(heads_low, full_out).astype(jnp.bfloat16),
                "mp",
                scatter_dimension=0,
                tiled=True,
            ).astype(jnp.float32)
            + b_out
        )
        first_norm, first_scaled, first_inverse = layer_norm(
            own_rows.astype(jnp.float32) + attention, norm1_gain, norm1_shift
        )
        first_low = first_norm.astype(jnp.bfloat16)
        normed_rows = lax.all_gather(first_low, "mp", axis=0, tiled=True)
        preact = product(normed_rows, full_up) + b_up
        active = jax.nn.gelu(preact, approximate=False).astype(jnp.bfloat16)
        ffn_out = (
            lax.psum_scatter(
                product(active, full_down).astype(jnp.bfloat16),
                "mp",
                scatter_dimension=0,
                tiled=True,
            ).astype(jnp.float32)
            + b_down
        )
        stream = first_norm + ffn_out
        final_norm, final_scaled, final_inverse = layer_norm(stream, norm2_gain, norm2_shift)
        outputs.append(final_norm.astype(jnp.bfloat16))
        limits = jnp.sum(
            jnp.where(owners[:, None] == seq_ids[None, :], seq_lengths[None, :], 0), axis=1
        )
        valid_row = (places < limits).astype(jnp.float32)[:, None]
        squares = [
            squares[0] + jnp.sum(valid_row * stream * stream),
            squares[1] + jnp.sum(valid_row * attention * attention),
            squares[2] + jnp.sum(valid_row * ffn_out * ffn_out),
            squares[3] + jnp.sum(valid_row),
        ]
        backward_weights = (
            lax.all_gather(weight_shard[0], "dp", axis=0, tiled=True),
            lax.all_gather(weight_shard[1], "dp", axis=0, tiled=True),
            lax.all_gather(weight_shard[2], "dp", axis=0, tiled=True),
            lax.all_gather(weight_shard[3], "dp", axis=0, tiled=True),
            lax.all_gather(weight_shard[4], "dp", axis=0, tiled=True),
            lax.all_gather(weight_shard[5], "dp", axis=0, tiled=True),
        )
        back_query, back_key, back_value, back_out, back_up, back_down = backward_weights
        back_joined = jnp.concatenate([back_query, back_key, back_value], axis=1)
        upstream = cotangent[micro_idx].astype(jnp.float32)
        stream_grad, gain_part, shift_part = norm_back(
            upstream, final_scaled, final_inverse, norm2_gain
        )
        gain2_grad = gain2_grad + gain_part
        shift2_grad = shift2_grad + shift_part
        down_bias_grad = down_bias_grad + jnp.sum(stream_grad, axis=0)
        ffn_grad_rows = lax.all_gather(stream_grad.astype(jnp.bfloat16), "mp", axis=0, tiled=True)
        active_grad = contract_cols(ffn_grad_rows, back_down)
        down_wgrad = down_wgrad + contract_rows(active, ffn_grad_rows)
        preact_grad = active_grad * gelu_slope(preact)
        up_bias_grad = up_bias_grad + jnp.sum(preact_grad, axis=0)
        preact_low = preact_grad.astype(jnp.bfloat16)
        up_wgrad = up_wgrad + contract_rows(normed_rows, preact_low)
        first_grad = stream_grad + lax.psum_scatter(
            contract_cols(preact_low, back_up).astype(jnp.bfloat16),
            "mp",
            scatter_dimension=0,
            tiled=True,
        ).astype(jnp.float32)
        attn_grad, gain_part, shift_part = norm_back(
            first_grad, first_scaled, first_inverse, norm1_gain
        )
        gain1_grad = gain1_grad + gain_part
        shift1_grad = shift1_grad + shift_part
        out_bias_grad = out_bias_grad + jnp.sum(attn_grad, axis=0)
        attn_grad_rows = lax.all_gather(attn_grad.astype(jnp.bfloat16), "mp", axis=0, tiled=True)
        heads_grad = contract_cols(attn_grad_rows, back_out).astype(jnp.bfloat16)
        out_wgrad = out_wgrad + contract_rows(heads_low, attn_grad_rows)

        def backward_seq(packed):
            return attend_backward(
                packed[0],
                packed[1],
                packed[2],
                packed[3],
                packed[4],
                packed[5],
                block_rows,
                score_scale,
            )

        query_grad, key_grad, value_grad = lax.map(
            backward_seq,
            (queries, keys_all, values_all, seq_lengths, logsum, heads_grad.reshape(four_shape)),
        )
        query_grad = query_grad.reshape(row_count, head_cols)
        key_grad = key_grad.reshape(row_count, head_cols)
        value_grad = value_grad.reshape(row_count, head_cols)
        query_bias_grad = query_bias_grad + jnp.sum(query_grad, axis=0)
        value_bias_grad = value_bias_grad + jnp.sum(value_grad, axis=0)
        joined_low = jnp.concatenate([query_grad, key_grad, value_grad], axis=1).astype(
            jnp.bfloat16
        )
        joined_wgrad = joined_wgrad + contract_rows(gathered_rows, joined_low)
        input_grads.append(
            attn_grad
            + lax.psum_scatter(
                contract_cols(joined_low, back_joined).astype(jnp.bfloat16),
                "mp",
                scatter_dimension=0,
                tiled=True,
            ).astype(jnp.float32)
        )
    query_wgrad = joined_wgrad[:, :head_cols]
    key_wgrad = joined_wgrad[:, head_cols : 2 * head_cols]
    value_wgrad = joined_wgrad[:, 2 * head_cols :]
    owned = (
        *in_one_piece(
            (
                query_wgrad.astype(jnp.bfloat16),
                key_wgrad.astype(jnp.bfloat16),
                value_wgrad.astype(jnp.bfloat16),
            ),
            "dp",
            0,
            1,
        ),
        summed_on_arrival(out_wgrad.astype(jnp.bfloat16), "dp", 0),
        *in_one_piece((up_wgrad.astype(jnp.bfloat16), down_wgrad.astype(jnp.bfloat16)), "dp", 0, 1),
        summed_on_arrival(query_bias_grad.astype(jnp.bfloat16), "dp", 0),
        summed_on_arrival(value_bias_grad.astype(jnp.bfloat16), "dp", 0),
        summed_on_arrival(up_bias_grad.astype(jnp.bfloat16), "dp", 0),
    )
    vectors = (
        lax.psum_scatter(out_bias_grad, ("dp", "mp"), scatter_dimension=0, tiled=True),
        lax.psum_scatter(down_bias_grad, ("dp", "mp"), scatter_dimension=0, tiled=True),
        lax.psum_scatter(gain1_grad, ("dp", "mp"), scatter_dimension=0, tiled=True),
        lax.psum_scatter(shift1_grad, ("dp", "mp"), scatter_dimension=0, tiled=True),
        lax.psum_scatter(gain2_grad, ("dp", "mp"), scatter_dimension=0, tiled=True),
        lax.psum_scatter(shift2_grad, ("dp", "mp"), scatter_dimension=0, tiled=True),
    )
    totals = lax.psum((squares[0], squares[1], squares[2], squares[3]), ("dp", "mp"))
    rms_values = jnp.sqrt(jnp.stack([totals[0], totals[1], totals[2]]) / (totals[3] * model_width))
    return (
        jnp.stack(outputs),
        jnp.stack(input_grads),
        owned[0],
        owned[1],
        owned[2],
        owned[3],
        owned[4],
        owned[5],
        owned[6],
        owned[7],
        owned[8],
        vectors[0],
        vectors[1],
        vectors[2],
        vectors[3],
        vectors[4],
        vectors[5],
        rms_values,
    )


def solution(mesh):
    return jax.shard_map(
        body,
        mesh=mesh,
        in_specs=(
            P(None, ("dp", "mp"), None),
            P(None, ("dp", "mp"), None),
            P(None, "dp"),
            P("dp", "mp"),
            P("dp", "mp"),
            P("dp", "mp"),
            P(("mp", "dp"), None),
            P("dp", "mp"),
            P(("mp", "dp"), None),
            P("mp"),
            P("mp"),
            P("mp"),
            P(),
            P(),
            P(),
            P(),
            P(),
            P(),
        ),
        out_specs=(
            P(None, ("dp", "mp"), None),
            P(None, ("dp", "mp"), None),
            P("dp", "mp"),
            P("dp", "mp"),
            P("dp", "mp"),
            P(("mp", "dp"), None),
            P("dp", "mp"),
            P(("mp", "dp"), None),
            P(("mp", "dp")),
            P(("mp", "dp")),
            P(("mp", "dp")),
            P(("dp", "mp")),
            P(("dp", "mp")),
            P(("dp", "mp")),
            P(("dp", "mp")),
            P(("dp", "mp")),
            P(("dp", "mp")),
            P(),
        ),
        check_vma=False,
    )
```

profile of v0, /device:TPU:0, one launch (start us, length us, event | category | flops | bytes accessed | tf_op | source)
XLA Modules:
  0.0 1063.6 jit_solution(8850179024312684034)
XLA Ops:
  14.9 34.7 %all_gather.64 = bf16[192,768]{1,0:T(8,128)(2,1)} all-gather(bf16[24,768]{1,0:T(8,128)(2,1)S(1)} %copy-done.76), channel_id=1, replica_groups=mesh['dp'=8,'mp'=4] {'dp'}, dimensions={0}, use_global_device_ids=true | all-gather | bytes 331776 | tf_op jit(solution)/shard_map/all_gather | solution.py:208
  49.6 31.1 %all_gather.28 = bf16[768,192]{1,0:T(8,128)(2,1)S(1)} all-gather(bf16[96,192]{1,0:T(8,128)(2,1)S(1)} %copy-done.73), channel_id=1, replica_groups=mesh['dp'=8,'mp'=4] {'dp'}, dimensions={0}, use_global_device_ids=true | all-gather | bytes 331776 | tf_op jit(solution)/shard_map/all_gather | solution.py:205
  80.7 31.3 %all_gather.29 = bf16[768,192]{1,0:T(8,128)(2,1)S(1)} all-gather(bf16[96,192]{1,0:T(8,128)(2,1)S(1)} %copy-done.74), channel_id=1, replica_groups=mesh['dp'=8,'mp'=4] {'dp'}, dimensions={0}, use_global_device_ids=true | all-gather | bytes 331776 | tf_op jit(solution)/shard_map/all_gather | solution.py:206
  112.0 31.0 %all_gather.30 = bf16[768,192]{1,0:T(8,128)(2,1)S(1)} all-gather(bf16[96,192]{1,0:T(8,128)(2,1)S(1)} %copy-done.75), channel_id=1, replica_groups=mesh['dp'=8,'mp'=4] {'dp'}, dimensions={0}, use_global_device_ids=true | all-gather | bytes 331776 | tf_op jit(solution)/shard_map/all_gather | solution.py:207
  171.0 46.0 %while.109 = (s32[]{:T(128)}, bf16[2,1024,3,64]{3,2,1,0:T(4,128)(2,1)S(1)}, f32[2,2,3,512]{3,2,1,0:T(4,128)}, bf16[2,1024,3,64]{1,3,2,0:T(8,128)(2,1)}, bf16[2,1...) while((s32[]{:T(128)}, ...), condition=%wide.region_5.6_spmd, body=%wide.region_0.5_spmd.sunk | while | flops 421527040 | bytes 28731884 | solution.py:227
  173.8 17.6 %while.116 = (s32[]{:T(128)}, bf16[2,512,3,64]{1,3,2,0:T(8,128)(2,1)}, f32[2,3,512]{2,1,0:T(4,128)S(1)}, s32[2]{0:T(128)S(1)}, bf16[1024,3,64]{0,2,1:T(8,128)(2,...) while((s32[]{:T(128)}, ...), condition=%wide.region_4.4_spmd.clone, body=%wide.region_1.3_spmd.clone.sunk | while | flops 421527040 | bytes 23460076 | solution.py:100
  196.8 17.6 %while.116 = (s32[]{:T(128)}, bf16[2,512,3,64]{1,3,2,0:T(8,128)(2,1)}, f32[2,3,512]{2,1,0:T(4,128)S(1)}, s32[2]{0:T(128)S(1)}, bf16[1024,3,64]{0,2,1:T(8,128)(2,...) while((s32[]{:T(128)}, ...), condition=%wide.region_4.4_spmd.clone, body=%wide.region_1.3_spmd.clone.sunk | while | flops 421527040 | bytes 23460076 | solution.py:100
  223.3 42.2 %while.111 = (s32[]{:T(128)}, bf16[2,1024,3,64]{3,2,1,0:T(4,128)(2,1)}, f32[2,2,3,512]{3,2,1,0:T(4,128)S(1)}, bf16[2,1024,3,64]{1,3,2,0:T(8,128)(2,1)}, bf16[2,1...) while((s32[]{:T(128)}, ...), condition=%wide.region_17.18_spmd, body=%wide.region_12.17_spmd.sunk | while | flops 421527040 | bytes 24934836 | solution.py:227
  226.3 16.1 %while.117 = (s32[]{:T(128)}, bf16[2,512,3,64]{1,3,2,0:T(8,128)(2,1)S(1)}, f32[2,3,512]{2,1,0:T(4,128)S(1)}, s32[2]{0:T(128)S(1)}, bf16[1024,3,64]{0,2,1:T(8,128...) while((s32[]{:T(128)}, ...), condition=%wide.region_16.16_spmd.clone, body=%wide.region_13.15_spmd.clone.sunk | while | flops 421527040 | bytes 20314292 | solution.py:100
  247.3 16.1 %while.117 = (s32[]{:T(128)}, bf16[2,512,3,64]{1,3,2,0:T(8,128)(2,1)S(1)}, f32[2,3,512]{2,1,0:T(4,128)S(1)}, s32[2]{0:T(128)S(1)}, bf16[1024,3,64]{0,2,1:T(8,128...) while((s32[]{:T(128)}, ...), condition=%wide.region_16.16_spmd.clone, body=%wide.region_13.15_spmd.clone.sunk | while | flops 421527040 | bytes 20314292 | solution.py:100
  277.3 36.0 %reduce-scatter.13.cloned.1.call-done = bf16[512,768]{1,0:T(8,128)(2,1)} async-done(((bf16[2048,768]{1,0:T(8,128)(2,1)}), bf16[512,768]{1,0:T(8,128)(2,1)}) %reduce-scatter.13.cloned.1.call-update) | async-done | bytes 786448 | tf_op jit(solution)/shard_map/reduce_scatter | solution.py:230
  319.4 28.7 %all-gather.19.cloned.1.call-done = bf16[2048,768]{1,0:T(8,128)(2,1)} async-done(((bf16[512,768]{1,0:T(8,128)(2,1)}), bf16[2048,768]{1,0:T(8,128)(2,1)}) %all-gather.19.cloned.1.call-update) | async-done | bytes 3145744 | tf_op jit(solution)/shard_map/all_gather | solution.py:242
  348.1 7.5 fusion.205
  355.6 22.9 %all-gather.13.cloned.1.call-done = bf16[2048,768]{1,0:T(8,128)(2,1)} async-done(((bf16[512,768]{1,0:T(8,128)(2,1)}), bf16[2048,768]{1,0:T(8,128)(2,1)}) %all-gather.13.cloned.1.call-update) | async-done | bytes 3145744 | tf_op jit(solution)/shard_map/all_gather | solution.py:242
  378.6 32.8 %fusion.82 = (bf16[2048,768]{1,0:T(8,128)(2,1)}, bf16[2048,768]{1,0:T(8,128)(2,1)}, f32[2048,768]{1,0:T(8,128)}) fusion(f32[768]{0:T(1024)S(1)} %copy-done.106, f32[2048,768]{1,0:T(8,128)} %fusion.205, bf16[2048,768]{1,0:T(8,128)(2,1)} %all-gather.13.cloned.1.call-done, bf16[768,768]{1,0:T(8,128)(2,1)} %all-gather.15.cloned.1.call-done), kind=kOutput, calls=%fused_computation.126 | convolution fusion | flops 2623537152 | bytes 23202816 | tf_op jit(solution)/shard_map/dot_general | solution.py:38
  411.3 10.9 %all-gather.17.cloned.1.call-done = bf16[768,768]{1,0:T(8,128)(2,1)} async-done(((bf16[96,768]{1,0:T(8,128)(2,1)}), bf16[768,768]{1,0:T(8,128)(2,1)}) %all-gather.17.cloned.1.call-update) | async-done | bytes 1179664 | tf_op jit(solution)/shard_map/all_gather | solution.py:210
  436.8 28.2 %reduce-scatter.11.cloned.1.call-done = bf16[512,768]{1,0:T(8,128)(2,1)} async-done(((bf16[2048,768]{1,0:T(8,128)(2,1)}), bf16[512,768]{1,0:T(8,128)(2,1)}) %reduce-scatter.11.cloned.1.call-update) | async-done | bytes 786448 | tf_op jit(solution)/shard_map/reduce_scatter | solution.py:246
  465.0 40.3 %reduce-scatter.15.cloned.1.call-done = bf16[512,768]{1,0:T(8,128)(2,1)} async-done(((bf16[2048,768]{1,0:T(8,128)(2,1)}), bf16[512,768]{1,0:T(8,128)(2,1)}) %reduce-scatter.15.cloned.1.call-update) | async-done | bytes 786448 | tf_op jit(solution)/shard_map/reduce_scatter | solution.py:246
  519.4 28.0 %all-gather.25.cloned.1.call-done = bf16[2048,768]{1,0:T(8,128)(2,1)} async-done(((bf16[512,768]{1,0:T(8,128)(2,1)}), bf16[2048,768]{1,0:T(8,128)(2,1)}) %all-gather.25.cloned.1.call-update) | async-done | bytes 3145744 | tf_op jit(solution)/shard_map/all_gather | solution.py:284
  560.5 16.9 %all-gather.21.cloned.1.call-done = bf16[2048,768]{1,0:T(8,128)(2,1)} async-done(((bf16[512,768]{1,0:T(8,128)(2,1)}), bf16[2048,768]{1,0:T(8,128)(2,1)}) %all-gather.21.cloned.1.call-update) | async-done | bytes 3145744 | tf_op jit(solution)/shard_map/all_gather | solution.py:284
  577.4 7.4 fusion.203
  590.6 7.7 reduce-scatter.21.cloned.1.call-done
  598.2 40.1 %reduce-scatter.17.cloned.1.call-done = bf16[512,768]{1,0:T(8,128)(2,1)} async-done(((bf16[2048,768]{1,0:T(8,128)(2,1)}), bf16[512,768]{1,0:T(8,128)(2,1)}) %reduce-scatter.17.cloned.1.call-update) | async-done | bytes 786448 | tf_op jit(solution)/shard_map/reduce_scatter | solution.py:291
  682.4 25.9 %all-gather.27.cloned.1.call-done = bf16[2048,768]{1,0:T(8,128)(2,1)} async-done(((bf16[512,768]{1,0:T(8,128)(2,1)}), bf16[2048,768]{1,0:T(8,128)(2,1)}) %all-gather.27.cloned.1.call-update) | async-done | bytes 3145744 | tf_op jit(solution)/shard_map/all_gather | solution.py:303
  716.9 70.3 %while.115 = (s32[]{:T(128)}, f32[2,1024,3,64]{3,2,1,0:T(4,128)}, bf16[2,1024,3,64]{1,3,2,0:T(8,128)(2,1)}, f32[2,1024,3,64]{1,3,2,0:T(8,128)}, f32[2,2,3,512]{3...) while((s32[]{:T(128)}, f32[2,1024,3,64]{3,2,1,0:T(4,128)}, ...), condition=%wide.region_44.45_spmd, body=%wide.region_40.44_spmd.sunk | while | flops 1031306752 | bytes 94972680 | solution.py:319
  721.6 23.5 %while.119 = (s32[]{:T(128)}, f32[1024,3,64]{0,2,1:T(8,128)S(1)}, f32[1024,3,64]{0,2,1:T(8,128)}, f32[2,512,3,64]{1,3,2,0:T(8,128)S(1)}, s32[2]{0:T(128)S(1)}, /...) while((s32[]{:T(128)}, f32[1024,3,64]{0,2,1:T(8,128)S(1)}, ...), condition=%wide.region_43.43_spmd.clone, body=%wide.region_41.42_spmd.clone.sunk | while | flops 1031306752 | bytes 59033876 | solution.py:145
  756.8 23.5 %while.119 = (s32[]{:T(128)}, f32[1024,3,64]{0,2,1:T(8,128)S(1)}, f32[1024,3,64]{0,2,1:T(8,128)}, f32[2,512,3,64]{1,3,2,0:T(8,128)S(1)}, s32[2]{0:T(128)S(1)}, /...) while((s32[]{:T(128)}, f32[1024,3,64]{0,2,1:T(8,128)S(1)}, ...), condition=%wide.region_43.43_spmd.clone, body=%wide.region_41.42_spmd.clone.sunk | while | flops 1031306752 | bytes 59033876 | solution.py:145
  811.1 71.9 %while.113 = (s32[]{:T(128)}, f32[2,1024,3,64]{3,2,1,0:T(4,128)}, bf16[2,1024,3,64]{1,3,2,0:T(8,128)(2,1)}, f32[2,1024,3,64]{1,3,2,0:T(8,128)}, f32[2,2,3,512]{3...) while((s32[]{:T(128)}, f32[2,1024,3,64]{3,2,1,0:T(4,128)}, ...), condition=%wide.region_33.34_spmd, body=%wide.region_29.33_spmd.sunk | while | flops 1031306752 | bytes 94972680 | solution.py:319
  816.7 23.5 %while.118 = (s32[]{:T(128)}, f32[1024,3,64]{0,2,1:T(8,128)S(1)}, f32[1024,3,64]{0,2,1:T(8,128)}, f32[2,512,3,64]{1,3,2,0:T(8,128)S(1)}, s32[2]{0:T(128)S(1)}, /...) while((s32[]{:T(128)}, f32[1024,3,64]{0,2,1:T(8,128)S(1)}, ...), condition=%wide.region_32.32_spmd.clone, body=%wide.region_30.31_spmd.clone.sunk | while | flops 1031306752 | bytes 59033876 | solution.py:145
  852.6 23.5 %while.118 = (s32[]{:T(128)}, f32[1024,3,64]{0,2,1:T(8,128)S(1)}, f32[1024,3,64]{0,2,1:T(8,128)}, f32[2,512,3,64]{1,3,2,0:T(8,128)S(1)}, s32[2]{0:T(128)S(1)}, /...) while((s32[]{:T(128)}, f32[1024,3,64]{0,2,1:T(8,128)S(1)}, ...), condition=%wide.region_32.32_spmd.clone, body=%wide.region_30.31_spmd.clone.sunk | while | flops 1031306752 | bytes 59033876 | solution.py:145
  926.2 23.7 %all-to-all-done.2 = bf16[8,96,1536]{2,1,0:T(8,128)(2,1)S(1)} async-done(((bf16[8,96,1536]{2,1,0:T(8,128)(2,1)}), bf16[8,96,1536]{2,1,0:T(8,128)(2,1)S(1)}, u32[]{:S(2)}, u32[]{:S(2)}) %all-to-all-start.2) | async-done | bytes 2359328 | tf_op jit(solution)/shard_map/all_to_all | solution.py:24
  997.0 42.3 %all-reduce.6 = (f32[768]{0:T(1024)S(1)}, f32[768]{0:T(1024)S(1)}, f32[768]{0:T(1024)S(1)}, f32[768]{0:T(1024)S(1)}, f32[768]{0:T(1024)S(1)}, /*index=5*/f32[768...) all-reduce(f32[768]{0:T(1024)S(1)} %add.427, ...), channel_id=12, replica_groups=mesh['dp'=8,'mp'=4] {'dp','mp'}, use_global_device_ids=true, to_apply=%region_60.61.clone | all-reduce | flops 4612 | bytes 36896
  (692 shorter events, 480.9 us)
Async XLA Ops:
  8.0 135.4 %all-gather.31.cloned.1.call-start = ((), (), s32[]{:S(2)}) async-start(), calls=%async_computation.31 | async-start | bytes 3932160 | tf_op jit(solution)/shard_map/all_gather | solution.py:216
  10.7 142.9 %all-gather.29.cloned.1.call-start = ((), (), s32[]{:S(2)}) async-start(), calls=%async_computation.30 | async-start | bytes 3932160 | tf_op jit(solution)/shard_map/all_gather | solution.py:216
  11.5 263.6 %reduce-scatter.9.cloned.1.call-start = ((), (), s32[]{:S(2)}) async-start(), calls=%async_computation.14 | async-start | bytes 3932160 | tf_op jit(solution)/shard_map/reduce_scatter | solution.py:230
  11.6 69.1 %copy-start.74 = (bf16[96,192]{1,0:T(8,128)(2,1)S(1)}, bf16[96,192]{1,0:T(8,128)(2,1)}, u32[]{:S(2)}) copy-start(bf16[96,192]{1,0:T(8,128)(2,1)} %param.38) | copy-start | bytes 110596
  13.4 98.5 %copy-start.75 = (bf16[96,192]{1,0:T(8,128)(2,1)S(1)}, bf16[96,192]{1,0:T(8,128)(2,1)}, u32[]{:S(2)}) copy-start(bf16[96,192]{1,0:T(8,128)(2,1)} %param.39) | copy-start | bytes 110596
  13.4 129.5 %copy-start.99 = (s32[2,2]{1,0:T(2,128)S(1)}, s32[2,2]{1,0:T(2,128)}, u32[]{:S(2)}) copy-start(s32[2,2]{1,0:T(2,128)} %param.36) | copy-start | bytes 52
  80.7 72.9 %copy-start.57 = (bf16[768,192]{1,0:T(8,128)(2,1)}, bf16[768,192]{1,0:T(8,128)(2,1)S(1)}, u32[]{:S(2)}) copy-start(bf16[768,192]{1,0:T(8,128)(2,1)S(1)} %all_gather.28) | copy-start | bytes 884740
  222.7 90.6 %reduce-scatter.13.cloned.1.call-start = ((), (), s32[]{:S(2)}) async-start(), calls=%async_computation.19 | async-start | bytes 3932160 | tf_op jit(solution)/shard_map/reduce_scatter | solution.py:230
  274.4 45.0 %all-gather.15.cloned.1.call-start = ((), (), s32[]{:S(2)}) async-start(), calls=%async_computation.16 | async-start | bytes 1327104 | tf_op jit(solution)/shard_map/all_gather | solution.py:209
  275.0 73.2 %all-gather.19.cloned.1.call-start = ((), (), s32[]{:S(2)}) async-start(), calls=%async_computation.20 | async-start | bytes 3932160 | tf_op jit(solution)/shard_map/all_gather | solution.py:242
  318.0 60.5 %all-gather.13.cloned.1.call-start = ((), (), s32[]{:S(2)}) async-start(), calls=%async_computation.15 | async-start | bytes 3932160 | tf_op jit(solution)/shard_map/all_gather | solution.py:242
  318.6 103.6 %all-gather.17.cloned.1.call-start = ((), (), s32[]{:S(2)}) async-start(), calls=%async_computation.17 | async-start | bytes 1327104 | tf_op jit(solution)/shard_map/all_gather | solution.py:210
  319.3 59.2 %copy-start.106 = (f32[768]{0:T(1024)S(1)}, f32[768]{0:T(1024)}, u32[]{:S(2)}) copy-start(f32[768]{0:T(1024)} %param.45) | copy-start | bytes 9220
  319.3 145.7 %reduce-scatter.11.cloned.1.call-start = ((), (), s32[]{:S(2)}) async-start(), calls=%async_computation.18 | async-start | bytes 3932160 | tf_op jit(solution)/shard_map/reduce_scatter | solution.py:246
  428.8 76.5 %reduce-scatter.15.cloned.1.call-start = ((), (), s32[]{:S(2)}) async-start(), calls=%async_computation.21 | async-start | bytes 3932160 | tf_op jit(solution)/shard_map/reduce_scatter | solution.py:246
  435.5 69.8 %copy-start.77 = (f32[768]{0:T(1024)S(1)}, f32[768]{0:T(1024)}, u32[]{:S(2)}) copy-start(f32[768]{0:T(1024)} %param.47) | copy-start | bytes 9220
  435.5 112.0 %all-gather.25.cloned.1.call-start = ((), (), s32[]{:S(2)}) async-start(), calls=%async_computation.26 | async-start | bytes 3932160 | tf_op jit(solution)/shard_map/all_gather | solution.py:284
  518.8 58.6 %all-gather.21.cloned.1.call-start = ((), (), s32[]{:S(2)}) async-start(), calls=%async_computation.22 | async-start | bytes 3932160 | tf_op jit(solution)/shard_map/all_gather | solution.py:284
  519.4 78.8 %reduce-scatter.21.cloned.1.call-start = ((), (), s32[]{:S(2)}) async-start(), calls=%async_computation.27 | async-start | bytes 3932160 | tf_op jit(solution)/shard_map/reduce_scatter | solution.py:291
  560.4 78.0 %reduce-scatter.17.cloned.1.call-start = ((), (), s32[]{:S(2)}) async-start(), calls=%async_computation.23 | async-start | bytes 3932160 | tf_op jit(solution)/shard_map/reduce_scatter | solution.py:291
  590.5 87.1 %all-gather.23.cloned.1.call-start = ((), (), s32[]{:S(2)}) async-start(), calls=%async_computation.24 | async-start | bytes 3932160 | tf_op jit(solution)/shard_map/all_gather | solution.py:303
  649.0 59.3 %all-gather.27.cloned.1.call-start = ((), (), s32[]{:S(2)}) async-start(), calls=%async_computation.28 | async-start | bytes 3932160 | tf_op jit(solution)/shard_map/all_gather | solution.py:303
  669.7 220.2 %all-to-all-start.5 = ((bf16[8,1,96]{2,1,0:T(2,128)(2,1)}), bf16[8,1,96]{2,1,0:T(2,128)(2,1)}, u32[]{:S(2)}, u32[]{:S(2)}) async-start(bf16[8,1,96]{2,1,0:T(2,128)(2,1)} %convert_element_type.314), calls=%async_computation.13 | async-start | bytes 8192 | tf_op jit(solution)/shard_map/all_to_all | solution.py:24
  675.2 374.7 %reduce-scatter.23.cloned.1.call-start = ((), (), s32[]{:S(2)}) async-start(), calls=%async_computation.29 | async-start | bytes 3932160 | tf_op jit(solution)/shard_map/reduce_scatter | solution.py:334
  889.8 60.0 %all-to-all-start.2 = ((bf16[8,96,1536]{2,1,0:T(8,128)(2,1)}), bf16[8,96,1536]{2,1,0:T(8,128)(2,1)S(1)}, u32[]{:S(2)}, u32[]{:S(2)}) async-start(bf16[8,96,1536]{2,1,0:T(8,128)(2,1)} %bitcast.47), calls=%async_computation.10 | async-start | bytes 4718592 | tf_op jit(solution)/shard_map/all_to_all | solution.py:24
  895.6 156.7 %reduce-scatter.19.cloned.1.call-start = ((), (), s32[]{:S(2)}) async-start(), calls=%async_computation.25 | async-start | bytes 3932160 | tf_op jit(solution)/shard_map/reduce_scatter | solution.py:334
  949.9 10.1 all-to-all-start.4
  959.9 9.7 all-to-all-start.3
  969.6 11.9 %all-to-all-start.1 = ((bf16[8,24,768]{2,1,0:T(8,128)(2,1)}), bf16[8,24,768]{2,1,0:T(8,128)(2,1)S(1)}, u32[]{:S(2)}, u32[]{:S(2)}) async-start(bf16[8,24,768]{2,1,0:T(8,128)(2,1)} %bitcast.46), calls=%async_computation.9 | async-start | bytes 589824 | tf_op jit(solution)/shard_map/all_to_all | solution.py:24
  981.5 66.2 %all-to-all-start = ((bf16[8,96,576]{2,1,0:T(8,128)(2,1)}), bf16[8,96,576]{2,1,0:T(8,128)(2,1)}, u32[]{:S(2)}, u32[]{:S(2)}) async-start(bf16[8,96,576]{2,1,0:T(8,128)(2,1)} %bitcast.45), calls=%async_computation.8 | async-start | bytes 1966080 | tf_op jit(solution)/shard_map/all_to_all | solution.py:24
  994.2 55.7 %copy-start.21 = (f32[512,768]{1,0:T(8,128)S(1)}, f32[512,768]{1,0:T(8,128)}, u32[]{:S(2)}) copy-start(f32[512,768]{1,0:T(8,128)} %get-tuple-element.940) | copy-start | bytes 4718596
  995.4 56.9 %copy-start.19 = (f32[512,768]{1,0:T(8,128)S(1)}, f32[512,768]{1,0:T(8,128)}, u32[]{:S(2)}) copy-start(f32[512,768]{1,0:T(8,128)} %copy-done.18) | copy-start | bytes 4718596
  (134 other events, 681.6 us)
Sparse Core Ops, SparseCore 0:
  10.8 31.2 all-gather.30
  44.2 28.4 all-gather.28
  222.8 38.7 reduce-scatter.8
  274.5 38.7 reduce-scatter.12
  518.9 28.4 all-gather.24
  548.9 28.4 all-gather.20
  649.1 28.4 all-gather.22
  679.8 28.4 all-gather.26
Sparse Core Ops, SparseCore 1:
  277.1 42.3 all-gather.14
  321.4 26.7 all-gather.18
  350.1 28.3 all-gather.12
  380.8 41.4 all-gather.16
  428.9 36.1 reduce-scatter.10
  467.6 37.7 reduce-scatter.14
  560.5 37.7 reduce-scatter.20
  600.6 37.7 reduce-scatter.16
  807.3 37.7 reduce-scatter.22
  915.6 38.1 reduce-scatter.18
where the time goes:
time: 1070 us; the launch traced here: 1060 us
  waiting for transfers between devices  323 us (30%)
  matrix products  218 us (20%)
  local copies, waits for them, and re-layouts  172 us (16%)
  blocking collectives  170 us (16%)
  other arithmetic  95.9 us (9%)
  loops' own time  32.2 us (3%)
  starting transfers between devices  28.9 us (3%)
  between operations  23 us (2%)
    reduce_scatter x2, waiting for transfers between devices, body(): lax.psum_scatter(product(active, full_down).astype(jnp.bfloat16), 'mp', s...  68.5 us
    dot_general x8, matrix products, product(): return jnp.dot(left_side, right_side, preferred_element_type=jnp.float32)  67.8 us
    all_gather x2, waiting for transfers between devices, body(): normed_rows = lax.all_gather(first_low, 'mp', axis=0, tiled=True)  51.7 us
    reduce_scatter x2, waiting for transfers between devices, body(): lax.psum_scatter(contract_cols(preact_low, back_up).astype(jnp.bfloat16),...  47.8 us
    all_gather x2, waiting for transfers between devices, body(): lax.all_gather(stream_grad.astype(jnp.bfloat16), 'mp', axis=0, tiled=True)  45 us
    unnamed x1, blocking collectives  42.3 us
    dot_general x8, matrix products, contract_cols(): lax.dot_general(left_side, right_side, (((1,), (1,)), ((), ())), preferre...  38.2 us
    reduce_scatter x2, waiting for transfers between devices, body(): lax.psum_scatter(product(heads_low, full_out).astype(jnp.bfloat16), 'mp',...  36 us
  transfers between devices with their start and end apart: 24, of which 15 were waited for; matrix products, arithmetic and copies ran while one was open for 34% of the time, Pallas kernels for 0%

commit v1 on v0

v1 whole, which is shorter than its diff:
```python
import functools

import jax
import jax.numpy as jnp
from jax import lax
from jax.experimental import pallas as pl
from jax.experimental.pallas import tpu as pltpu
from jax.sharding import PartitionSpec as P

HD = 64
L = 1024
SEQ_MB = 2
MB = 2
GROUPS = 4
GH = 3
GC = GH * HD
PAD = 256

epsilon = 1e-05
masked_score = -1e30
exp2_scale = HD ** (-0.5) * 1.4426950408889634
score_scale = HD ** (-0.5)
BOTH = ("dp", "mp")
NT = (((1,), (1,)), ((), ()))


def product(left_side, right_side):
    return jnp.dot(left_side, right_side, preferred_element_type=jnp.float32)


def contract_rows(left_side, right_side):
    return lax.dot_general(
        left_side, right_side, (((0,), (0,)), ((), ())), preferred_element_type=jnp.float32
    )


def contract_cols(left_side, right_side):
    return lax.dot_general(left_side, right_side, NT, preferred_element_type=jnp.float32)


def layer_norm(values, norm_gain, norm_shift):
    center = values - jnp.mean(values, axis=-1, keepdims=True)
    spread = jnp.mean(center * center, axis=-1, keepdims=True)
    inverse = lax.rsqrt(spread + epsilon)
    scaled = center * inverse
    return (scaled * norm_gain + norm_shift, scaled, inverse)


def norm_back(upstream, scaled, inverse, norm_gain):
    gain_grad = jnp.sum(upstream * scaled, axis=0)
    shift_grad = jnp.sum(upstream, axis=0)
    through = upstream * norm_gain
    result = inverse * (
        through
        - jnp.mean(through, axis=-1, keepdims=True)
        - scaled * jnp.mean(through * scaled, axis=-1, keepdims=True)
    )
    return (result, gain_grad, shift_grad)


def head_keys(keys, bias, h, lane):
    kept = jnp.where((lane >= h * HD) & (lane < (h + 1) * HD), keys, jnp.zeros_like(keys))
    return jnp.where(lane == GC, bias, kept)


def attend_forward_kernel(bias_ref, qkv_ref, out_ref, lse_ref, turned):
    rows = qkv_ref.shape[1]
    chunk = 256
    lane = lax.broadcasted_iota(jnp.int32, (1, PAD), 1)
    keys = qkv_ref[0, :, PAD : 2 * PAD]
    values_t = qkv_ref[0, :, 2 * PAD :].T
    bias = bias_ref[...]
    for h in range(GH):
        own = head_keys(keys, bias, h, lane)
        own_values = values_t[h * HD : (h + 1) * HD, :]
        for at in range(0, rows, chunk):
            queries = qkv_ref[0, at : at + chunk, :PAD]
            scores = contract_cols(own, queries)
            top = jnp.max(scores, axis=0, keepdims=True) * exp2_scale
            raised = jnp.exp2(scores * exp2_scale - top)
            total = jnp.sum(raised, axis=0, keepdims=True)
            mixed = product(own_values, raised.astype(jnp.bfloat16))
            turned[h * HD : (h + 1) * HD, at : at + chunk] = mixed / total
            lse_ref[0, h : h + 1, at : at + chunk] = top + jnp.log2(total)
    turned[GC:, :] = jnp.zeros((PAD - GC, rows), jnp.float32)
    out_ref[0] = turned[...].T.astype(jnp.bfloat16)


def attend_forward(qkv, bias):
    rows = qkv.shape[1]
    return pl.pallas_call(
        attend_forward_kernel,
        grid=(GROUPS,),
        in_specs=[
            pl.BlockSpec((rows, 1), lambda g: (0, 0)),
            pl.BlockSpec((1, rows, 3 * PAD), lambda g: (g, 0, 0)),
        ],
        out_specs=[
            pl.BlockSpec((1, rows, PAD), lambda g: (g, 0, 0)),
            pl.BlockSpec((1, 8, rows), lambda g: (g, 0, 0)),
        ],
        out_shape=[
            jax.ShapeDtypeStruct((GROUPS, rows, PAD), jnp.bfloat16),
            jax.ShapeDtypeStruct((GROUPS, 8, rows), jnp.float32),
        ],
        scratch_shapes=[pltpu.VMEM((PAD, rows), jnp.float32)],
        cost_estimate=pl.CostEstimate(
            flops=45_000_000_000 // 3, bytes_accessed=10_000_000, transcendentals=12_000_000
        ),
    )(bias, qkv)


def attend_backward_kernel(
    bias_ref, qkv_ref, out_ref, lse_ref, grad_ref, joined_ref, sums_ref, probs, slopes, turned
):
    rows = qkv_ref.shape[1]
    chunk = 256
    lane = lax.broadcasted_iota(jnp.int32, (1, PAD), 1)
    keys = qkv_ref[0, :, PAD : 2 * PAD]
    keys_t = keys.T
    values = qkv_ref[0, :, 2 * PAD :]
    bias = bias_ref[...]
    crossed = (grad_ref[0].astype(jnp.float32) * out_ref[0].astype(jnp.float32)).T
    key_grad = jnp.zeros((rows, PAD), jnp.float32)
    value_grad = jnp.zeros((rows, PAD), jnp.float32)
    for h in range(GH):
        head = (lane >= h * HD) & (lane < (h + 1) * HD)
        own = head_keys(keys, bias, h, lane)
        own_values = jnp.where(head, values, jnp.zeros_like(values))
        delta = jnp.sum(crossed[h * HD : (h + 1) * HD, :], axis=0, keepdims=True)
        for at in range(0, rows, chunk):
            queries = qkv_ref[0, at : at + chunk, :PAD]
            grads = grad_ref[0, at : at + chunk, :]
            scores = contract_cols(own, queries)
            attn_probs = jnp.exp2(scores * exp2_scale - lse_ref[0, h : h + 1, at : at + chunk])
            prob_grad = contract_cols(own_values, grads)
            probs[:, at : at + chunk] = attn_probs.astype(jnp.bfloat16)
            slopes[:, at : at + chunk] = (
                attn_probs * (prob_grad - delta[:, at : at + chunk])
            ).astype(jnp.bfloat16)
        own_grads = jnp.where(head, grad_ref[0], jnp.zeros((), jnp.bfloat16))
        own_queries = jnp.where(head, qkv_ref[0, :, :PAD], jnp.zeros((), jnp.bfloat16))
        value_grad = value_grad + product(probs[...], own_grads)
        key_grad = key_grad + product(slopes[...], own_queries)
        turned[h * HD : (h + 1) * HD, :] = product(
            keys_t[h * HD : (h + 1) * HD, :], slopes[...]
        )
    turned[GC:, :] = jnp.zeros((PAD - GC, rows), jnp.float32)
    query_grad = turned[...].T * score_scale
    joined_ref[0, :, :PAD] = query_grad.astype(jnp.bfloat16)
    joined_ref[0, :, PAD : 2 * PAD] = (key_grad * score_scale).astype(jnp.bfloat16)
    joined_ref[0, :, 2 * PAD :] = value_grad.astype(jnp.bfloat16)
    sums_ref[0, 0:1, :] = jnp.sum(query_grad, axis=0, keepdims=True)
    sums_ref[0, 1:2, :] = jnp.sum(value_grad, axis=0, keepdims=True)


def attend_backward(qkv, bias, heads_out, lse, heads_grad):
    rows = qkv.shape[1]
    return pl.pallas_call(
        attend_backward_kernel,
        grid=(GROUPS,),
        in_specs=[
            pl.BlockSpec((rows, 1), lambda g: (0, 0)),
            pl.BlockSpec((1, rows, 3 * PAD), lambda g: (g, 0, 0)),
            pl.BlockSpec((1, rows, PAD), lambda g: (g, 0, 0)),
            pl.BlockSpec((1, 8, rows), lambda g: (g, 0, 0)),
            pl.BlockSpec((1, rows, PAD), lambda g: (g, 0, 0)),
        ],
        out_specs=[
            pl.BlockSpec((1, rows, 3 * PAD), lambda g: (g, 0, 0)),
            pl.BlockSpec((1, 8, PAD), lambda g: (g, 0, 0)),
        ],
        out_shape=[
            jax.ShapeDtypeStruct((GROUPS, rows, 3 * PAD), jnp.bfloat16),
            jax.ShapeDtypeStruct((GROUPS, 8, PAD), jnp.float32),
        ],
        scratch_shapes=[
            pltpu.VMEM((rows, rows), jnp.bfloat16),
            pltpu.VMEM((rows, rows), jnp.bfloat16),
            pltpu.VMEM((PAD, rows), jnp.float32),
        ],
        cost_estimate=pl.CostEstimate(
            flops=30_000_000_000, bytes_accessed=20_000_000, transcendentals=12_000_000
        ),
    )(bias, qkv, heads_out, lse, heads_grad)


def swap_with_partner(values):
    size = lax.axis_size("mp")
    return lax.ppermute(values, "mp", [(i, i ^ 1) for i in range(size)])


def pad_heads(values):
    return jnp.pad(values, [(0, 0)] * (values.ndim - 1) + [(0, PAD - values.shape[-1])])


MESH = pl.DeviceIdType.MESH


def positions():
    mp, dp = lax.axis_index("mp"), lax.axis_index("dp")
    return mp, lax.div(mp, 2), lax.rem(mp, 2), lax.div(dp, 2), lax.rem(dp, 2)


def at_place(x, c, z, y):
    return (2 * z + y, 2 * x + c)


def neighbours(nz):
    mp, x, c, z, y = positions()
    first = at_place(lax.rem(x + c, 2), c, z, lax.rem(y + 1 - c, 2))
    second = at_place(lax.rem(x + 1 - c, 2), c, z, lax.rem(y + c, 2))
    partner = at_place(x, 1 - c, z, y)
    along = [at_place(x, c, lax.rem(z + d, nz), y) for d in range(1, nz)]
    return first, second, partner, along


def meet(devices):
    barrier = pltpu.get_barrier_semaphore()
    for device in devices:
        pl.semaphore_signal(barrier, inc=1, device_id=device, device_id_type=MESH)
    pl.semaphore_wait(barrier, len(devices))


def regions(x, c, y):
    own = (x, y)
    first = (lax.rem(x + c, 2), lax.rem(y + 1 - c, 2))
    second = (lax.rem(x + 1 - c, 2), lax.rem(y + c, 2))
    third = (1 - x, 1 - y)
    return own, first, second, third


def gather_kernel(nz, parts, *refs):
    shards, fulls = refs[:parts], refs[parts : 2 * parts]
    own_sem, z_send, z_recv, send, recv = refs[2 * parts :]
    mp, x, c, z, y = positions()
    first, second, partner, along = neighbours(nz)
    meet([first, second, partner, *along])
    own, got1, got2, got3 = regions(x, c, y)
    other = regions(x, 1 - c, y)

    def remote(src, dst, s, r, device):
        return pltpu.make_async_remote_copy(
            src_ref=src, dst_ref=dst, send_sem=s, recv_sem=r, device_id=device, device_id_type=MESH
        )

    started = []
    locals_ = []
    spread = []
    for p in range(parts):
        keep = pltpu.make_async_copy(shards[p], fulls[p].at[x, c, z, y], own_sem.at[p])
        keep.start()
        locals_.append(keep)
        sends = [
            remote(shards[p], fulls[p].at[x, c, z, y], z_send.at[p, d], z_recv.at[p, d], along[d])
            for d in range(nz - 1)
        ]
        for copy in sends:
            copy.start()
        spread.append(sends)

    def block(p, core, place):
        return fulls[p].at[place[0], core, :, place[1]]

    def push(p, k, core, place, device):
        copy = remote(block(p, core, place), block(p, core, place), send.at[p, k], recv.at[p, k], device)
        copy.start()
        started.append(copy)
        return copy

    def arrived(p, k, core, place):
        here = block(p, core, place)
        remote(here, here, send.at[p, k], recv.at[p, k], first).wait_recv()

    for p in range(parts):
        locals_[p].wait()
        for copy in spread[p]:
            copy.wait_recv()
        push(p, 0, c, own, first)
        push(p, 1, c, own, second)
        push(p, 3, c, own, partner)
    for p in range(parts):
        arrived(p, 0, c, got1)
        push(p, 2, c, got1, second)
        push(p, 4, c, got1, partner)
    for p in range(parts):
        arrived(p, 1, c, got2)
        push(p, 5, c, got2, partner)
        arrived(p, 2, c, got3)
        push(p, 6, c, got3, partner)
    for p in range(parts):
        for k in range(4):
            arrived(p, 3 + k, 1 - c, other[k])
    for sends in spread:
        for copy in sends:
            copy.wait_send()
    for copy in started:
        copy.wait_send()


def gather_all(shards):
    n_dp = lax.axis_size("dp")
    nz, parts = n_dp // 2, len(shards)
    return pl.pallas_call(
        functools.partial(gather_kernel, nz, parts),
        in_specs=[pl.BlockSpec(memory_space=pltpu.VMEM)] * parts,
        out_specs=[pl.BlockSpec(memory_space=pl.ANY)] * parts,
        out_shape=[jax.ShapeDtypeStruct((2, 2, nz, 2, *s.shape), s.dtype) for s in shards],
        scratch_shapes=[
            pltpu.SemaphoreType.DMA((parts,)),
            pltpu.SemaphoreType.DMA((parts, nz - 1)),
            pltpu.SemaphoreType.DMA((parts, nz - 1)),
            pltpu.SemaphoreType.DMA((parts, 7)),
            pltpu.SemaphoreType.DMA((parts, 7)),
        ],
        compiler_params=pltpu.CompilerParams(collective_id=0, has_side_effects=True),
    )(*shards)


def scatter_kernel(nz, parts, *refs):
    partials, results = refs[:parts], refs[parts : 2 * parts]
    at = 2 * parts
    sums, heard1, heard2, heard3, heard4 = (
        refs[at + i * parts : at + (i + 1) * parts] for i in range(5)
    )
    own_sem, send, recv, z_send, z_recv = refs[at + 5 * parts :]
    mp, x, c, z, y = positions()
    first, second, partner, along = neighbours(nz)
    meet([first, second, partner, *along])
    own, got1, got2, got3 = regions(x, c, y)
    started = []

    def remote(src, dst, s, r, device):
        copy = pltpu.make_async_remote_copy(
            src_ref=src, dst_ref=dst, send_sem=s, recv_sem=r, device_id=device, device_id_type=MESH
        )
        copy.start()
        started.append(copy)
        return copy

    def add(p, place, more):
        for i in range(nz):
            here = sums[p].at[place[0], i, place[1]]
            here[...] = (here[...].astype(jnp.float32) + more[i].astype(jnp.float32)).astype(here.dtype)

    kept, core_copies = [], []
    for p in range(parts):
        copies = []
        for k in range(2):
            keep = pltpu.make_async_copy(partials[p].at[k, c], sums[p].at[k], own_sem.at[p, k])
            keep.start()
            copies.append(keep)
        kept.append(copies)
        core_copies.append(
            [
                remote(partials[p].at[k, 1 - c], heard1[p].at[k], send.at[p, k], recv.at[p, k], partner)
                for k in range(2)
            ]
        )
    second_copies = []
    for p in range(parts):
        for copy in kept[p]:
            copy.wait()
        for copy in core_copies[p]:
            copy.wait_recv()
        copies = []
        for k, place in enumerate((got2, got3)):
            add(p, place, heard1[p].at[place[0], :, place[1]])
            copies.append(
                remote(
                    sums[p].at[place[0], :, place[1]],
                    heard2[p].at[k],
                    send.at[p, 2 + k],
                    recv.at[p, 2 + k],
                    second,
                )
            )
        second_copies.append(copies)
        for place in (got1, own):
            add(p, place, heard1[p].at[place[0], :, place[1]])
    first_copies = []
    for p in range(parts):
        second_copies[p][1].wait_recv()
        add(p, got1, heard2[p].at[1])
        first_copies.append(
            remote(sums[p].at[got1[0], :, got1[1]], heard3[p], send.at[p, 4], recv.at[p, 4], first)
        )
        second_copies[p][0].wait_recv()
        add(p, own, heard2[p].at[0])
    last_copies = []
    for p in range(parts):
        first_copies[p].wait_recv()
        add(p, own, heard3[p])
        last_copies.append(
            [
                remote(
                    sums[p].at[x, lax.rem(z + d + 1, nz), y],
                    heard4[p].at[d],
                    z_send.at[p, d],
                    z_recv.at[p, d],
                    along[d],
                )
                for d in range(nz - 1)
            ]
        )
    for p in range(parts):
        for copy in last_copies[p]:
            copy.wait_recv()
        total = sums[p][x, z, y].astype(jnp.float32)
        for d in range(nz - 1):
            total = total + heard4[p][d].astype(jnp.float32)
        results[p][...] = total
    for copy in started:
        copy.wait_send()


def scatter_sums(partials):
    nz, parts = lax.axis_size("dp") // 2, len(partials)
    tails = [p.shape[4:] for p in partials]
    kinds = [p.dtype for p in partials]
    return pl.pallas_call(
        functools.partial(scatter_kernel, nz, parts),
        in_specs=[pl.BlockSpec(memory_space=pl.ANY)] * parts,
        out_specs=[pl.BlockSpec(memory_space=pltpu.VMEM)] * parts,
        out_shape=[jax.ShapeDtypeStruct(t, jnp.float32) for t in tails],
        scratch_shapes=[
            *[pltpu.VMEM((2, nz, 2, *t), k) for t, k in zip(tails, kinds)],
            *[pltpu.VMEM((2, nz, 2, *t), k) for t, k in zip(tails, kinds)],
            *[pltpu.VMEM((2, nz, *t), k) for t, k in zip(tails, kinds)],
            *[pltpu.VMEM((nz, *t), k) for t, k in zip(tails, kinds)],
            *[pltpu.VMEM((nz - 1, *t), k) for t, k in zip(tails, kinds)],
            pltpu.SemaphoreType.DMA((parts, 2)),
            pltpu.SemaphoreType.DMA((parts, 5)),
            pltpu.SemaphoreType.DMA((parts, 5)),
            pltpu.SemaphoreType.DMA((parts, nz - 1)),
            pltpu.SemaphoreType.DMA((parts, nz - 1)),
        ],
        compiler_params=pltpu.CompilerParams(
            collective_id=1, has_side_effects=True, vmem_limit_bytes=60 * 1024 * 1024
        ),
    )(*partials)


def in_place_order(blocks):
    return blocks.reshape(2, 2, blocks.shape[1] // 2, 2, *blocks.shape[2:])


def body(
    tokens,
    cotangent,
    lengths,
    w_query,
    w_key,
    w_value,
    w_out,
    w_up,
    w_down,
    b_query,
    b_value,
    b_up,
    b_out,
    b_down,
    norm1_gain,
    norm1_shift,
    norm2_gain,
    norm2_shift,
):
    half_rows = tokens.shape[1]
    width = tokens.shape[2]
    n_dp, n_mp = lax.axis_size("dp"), lax.axis_size("mp")
    unit_cols = w_up.shape[1]
    mp_index = lax.axis_index("mp")
    half = lax.rem(mp_index, 2)
    seq = lax.div(mp_index, 2)

    def own_of(pair):
        return jnp.where(half == 0, pair[0], pair[1])

    def other_of(pair):
        return jnp.where(half == 0, pair[1], pair[0])

    rows_in = jnp.concatenate([own_of(tokens), swap_with_partner(other_of(tokens))], axis=0)
    rows_cot = jnp.concatenate([own_of(cotangent), swap_with_partner(other_of(cotangent))], axis=0)
    length = lax.dynamic_slice(lengths, (half, seq), (1, 1))[0, 0]
    place = jnp.arange(half_rows, dtype=jnp.int32)
    place = jnp.concatenate([place + half * half_rows, place + (1 - half) * half_rows])
    valid_row = (place < length)[:, None]
    bias = jnp.where(valid_row, 0.0, masked_score).astype(jnp.bfloat16)
    valid_row = valid_row.astype(jnp.float32)

    biases = jnp.pad(jnp.concatenate([b_query, b_value, b_up]), (0, 896)).reshape(16, 128)
    qkv_shard = jnp.concatenate([w_query, w_key, w_value], axis=1)
    gathered = gather_all([qkv_shard, w_out, w_up, w_down, biases])
    full_qkv, full_out, full_up, full_down, full_bias = (
        g.reshape(n_mp, n_dp, *g.shape[4:]) for g in gathered
    )
    full_qkv = full_qkv.reshape(n_mp, width, 3, GC)
    w_joined = pad_heads(full_qkv).reshape(n_mp, width, 3 * PAD)
    full_out = full_out.reshape(n_mp, GC, width)
    out_pad = jnp.pad(full_out, ((0, 0), (0, PAD - GC), (0, 0))).reshape(n_mp * PAD, width)
    full_up = full_up.reshape(n_mp, width, unit_cols).transpose(1, 0, 2).reshape(width, n_mp * unit_cols)
    full_down = full_down.reshape(n_mp * unit_cols, width)
    full_bias = full_bias[:, 0].reshape(n_mp, -1)
    bias_q, bias_v, bias_up = full_bias[:, :GC], full_bias[:, GC:2*GC], full_bias[:, 2*GC:2*GC+unit_cols]
    mark = jnp.zeros((n_mp, PAD - GC), jnp.float32).at[:, 0].set(1.0)
    joined_bias = jnp.concatenate(
        [bias_q, mark, jnp.zeros((n_mp, PAD), jnp.float32), pad_heads(bias_v)], axis=1
    )

    qkv = lax.dot_general(
        jnp.broadcast_to(rows_in[None], (n_mp, *rows_in.shape)),
        w_joined,
        (((2,), (1,)), ((0,), (0,))),
        preferred_element_type=jnp.float32,
    )
    qkv = (qkv + joined_bias[:, None, :]).astype(jnp.bfloat16)
    heads_out, lse = attend_forward(qkv, bias)
    heads_flat = heads_out.transpose(1, 0, 2).reshape(2 * half_rows, n_mp * PAD)
    attention = product(heads_flat, out_pad) + b_out
    first_norm, first_scaled, first_inverse = layer_norm(
        rows_in.astype(jnp.float32) + attention, norm1_gain, norm1_shift
    )
    first_low = first_norm.astype(jnp.bfloat16)
    preact = product(first_low, full_up) + bias_up.reshape(-1)
    cumulative = 0.5 * (1.0 + lax.erf(preact * 0.7071067811865476))
    active = (preact * cumulative).astype(jnp.bfloat16)
    slope = cumulative + preact * (jnp.exp(-0.5 * preact * preact) * 0.3989422804014327)
    ffn_out = product(active, full_down) + b_down
    stream = first_norm + ffn_out
    final_norm, final_scaled, final_inverse = layer_norm(stream, norm2_gain, norm2_shift)
    output = final_norm.astype(jnp.bfloat16)
    squares = jnp.stack(
        [
            jnp.sum(valid_row * stream * stream),
            jnp.sum(valid_row * attention * attention),
            jnp.sum(valid_row * ffn_out * ffn_out),
            jnp.sum(valid_row),
        ]
    )

    stream_grad, gain2_grad, shift2_grad = norm_back(
        rows_cot.astype(jnp.float32), final_scaled, final_inverse, norm2_gain
    )
    down_bias_grad = jnp.sum(stream_grad, axis=0)
    ffn_grad_low = stream_grad.astype(jnp.bfloat16)
    active_grad = contract_cols(ffn_grad_low, full_down)
    down_wgrad = contract_rows(active, ffn_grad_low)
    preact_grad = active_grad * slope
    up_bias_grad = jnp.sum(preact_grad, axis=0)
    preact_low = preact_grad.astype(jnp.bfloat16)
    up_wgrad = contract_rows(first_low, preact_low)
    first_grad = stream_grad + contract_cols(preact_low, full_up)
    attn_grad, gain1_grad, shift1_grad = norm_back(
        first_grad, first_scaled, first_inverse, norm1_gain
    )
    out_bias_grad = jnp.sum(attn_grad, axis=0)
    attn_grad_low = attn_grad.astype(jnp.bfloat16)
    out_wgrad = contract_rows(heads_flat, attn_grad_low)
    heads_grad = contract_cols(attn_grad_low, out_pad).astype(jnp.bfloat16)
    heads_grad = heads_grad.reshape(2 * half_rows, n_mp, PAD).transpose(1, 0, 2)
    joined, sums = attend_backward(qkv, bias, heads_out, lse, heads_grad)
    joined_wgrad = lax.dot_general(
        jnp.broadcast_to(rows_in[None], (n_mp, *rows_in.shape)),
        joined,
        (((1,), (1,)), ((0,), (0,))),
        preferred_element_type=jnp.float32,
    )
    tokens_grad = attn_grad + jnp.sum(
        lax.dot_general(
            joined, w_joined, (((2,), (2,)), ((0,), (0,))), preferred_element_type=jnp.float32
        ),
        axis=0,
    )

    low = jnp.bfloat16
    joined_blocks = (
        joined_wgrad.astype(low)
        .reshape(n_mp, n_dp, width // n_dp, 3, PAD)[..., :GC]
        .reshape(n_mp, n_dp, width // n_dp, 3 * GC)
    )
    out_blocks = (
        out_wgrad.astype(low)
        .reshape(n_mp, PAD, width)[:, :GC]
        .reshape(n_mp, n_dp, GC // n_dp, width)
    )
    up_blocks = up_wgrad.astype(low).reshape(n_dp, width // n_dp, n_mp, unit_cols).transpose(2, 0, 1, 3)
    down_blocks = down_wgrad.astype(low).reshape(n_mp, n_dp, unit_cols // n_dp, width)

    def by_mp(vector):
        return vector.reshape(n_mp, n_dp, -1)

    def by_dp(vector):
        return vector.reshape(n_dp, n_mp, -1).transpose(1, 0, 2)

    vectors = [by_mp(sums[:, 0, :GC]), by_mp(sums[:, 1, :GC]), by_mp(up_bias_grad)]
    vectors += [
        by_dp(v)
        for v in (out_bias_grad, down_bias_grad, gain1_grad, shift1_grad, gain2_grad, shift2_grad)
    ]
    vectors.append(jnp.broadcast_to(squares, (n_mp, n_dp, 4)))
    ends = [v.shape[-1] for v in vectors]
    vectors = jnp.concatenate(vectors, axis=-1)
    vectors = jnp.pad(vectors, ((0, 0), (0, 0), (0, 1024 - vectors.shape[-1])))
    vectors = vectors.reshape(n_mp, n_dp, 8, 128)
    own_down, own_up, own_out, own_joined, own_vector = scatter_sums(
        [
            in_place_order(b)
            for b in (down_blocks, up_blocks, out_blocks, joined_blocks, vectors)
        ]
    )
    own_vector = own_vector.reshape(-1)
    own_vectors, start = [], 0
    for size in ends:
        own_vectors.append(own_vector[start : start + size])
        start += size
    totals = own_vectors.pop()
    rms_values = jnp.sqrt(totals[:3] / (totals[3] * width))

    def back_home(rows):
        mine, sent = rows[:half_rows], swap_with_partner(rows[half_rows:])
        return jnp.where(half == 0, jnp.stack([mine, sent]), jnp.stack([sent, mine]))

    return (
        back_home(output),
        back_home(tokens_grad),
        own_joined[:, :GC],
        own_joined[:, GC : 2 * GC],
        own_joined[:, 2 * GC :],
        own_out,
        own_up,
        own_down,
        *own_vectors,
        rms_values,
    )


def solution(mesh):
    rows = P(None, BOTH, None)
    split, rows_split = P("dp", "mp"), P(("mp", "dp"), None)
    return jax.shard_map(
        body,
        mesh=mesh,
        in_specs=(
            rows,
            rows,
            P(None, "dp"),
            split,
            split,
            split,
            rows_split,
            split,
            rows_split,
            P("mp"),
            P("mp"),
            P("mp"),
            *([P()] * 6),
        ),
        out_specs=(
            rows,
            rows,
            split,
            split,
            split,
            rows_split,
            split,
            rows_split,
            *([P(("mp", "dp"))] * 3),
            *([P(BOTH)] * 6),
            P(),
        ),
        check_vma=False,
    )
```

time: 1070 us -> 533 us (0.50)
  waiting for transfers between devices: 323 us -> 0.01 us
  Pallas kernels: 0 us -> 265 us
  blocking collectives: 170 us -> 0 us
  matrix products: 218 us -> 99.4 us
  other arithmetic: 95.9 us -> 25.8 us
  local copies, waits for them, and re-layouts: 172 us -> 129 us
  loops' own time: 32.2 us -> 0 us
  starting transfers between devices: 28.9 us -> 1.5 us
  between operations: 23 us -> 2.96 us
    pallas_call x0 -> x4, Pallas kernels: none -> 265 us  [the longest x1 109 us: scatter_sums(): pl.pallas_call(functools.partial(scatter_kernel, nz, parts), in_specs=[pl...]
    reduce_scatter x8 -> x0, waiting for transfers between devices: 152 us -> none  [the longest x2 68.5 us: body(): lax.psum_scatter(product(active, full_down).astype(jnp.bfloat16), 'mp', s...]
    all_gather x10 -> x0, waiting for transfers between devices: 136 us -> none  [the longest x2 51.7 us: body(): normed_rows = lax.all_gather(first_low, 'mp', axis=0, tiled=True)]
    all_gather x4 -> x0, blocking collectives: 128 us -> none  [the longest x1 34.7 us: body(): lax.all_gather(weight_shard[3], 'dp', axis=0, tiled=True)]
    dot_general x64 -> x6, matrix products: 118 us -> 50.7 us  [the longest x3 24.8 us: contract_cols(): lax.dot_general(left_side, right_side, NT, preferred_element_type=jnp.flo...]
    dot_general x8 -> x3, matrix products: 67.8 us -> 25.5 us  [product(): return jnp.dot(left_side, right_side, preferred_element_type=jnp.float32)]
    unnamed x1 -> x0, blocking collectives: 42.3 us -> none
    while x112 -> x0, local copies, waits for them, and re-layouts: 38.7 us -> none
  transfers between devices with their start and end apart: 24 -> 4, of which waited for: 15 -> 0; matrix products, arithmetic and copies ran while one was open for 34% -> 32% of each run, Pallas kernels for 0% -> 44%
where the time goes in v1:
time: 533 us; the launch traced here: 523 us
  Pallas kernels  265 us (50%)
  local copies, waits for them, and re-layouts  129 us (24%)
  matrix products  99.4 us (19%)
  other arithmetic  25.8 us (5%)
    pallas_call x1, Pallas kernels, scatter_sums(): pl.pallas_call(functools.partial(scatter_kernel, nz, parts), in_specs=[pl...  109 us
    pallas_call x1, Pallas kernels, gather_all(): pl.pallas_call(functools.partial(gather_kernel, nz, parts), in_specs=[pl....  87.8 us
    pallas_call x1, Pallas kernels, attend_backward(): pl.pallas_call(attend_backward_kernel, grid=(GROUPS,), in_specs=[pl.Block...  36.5 us
    pallas_call x1, Pallas kernels, attend_forward(): pl.pallas_call(attend_forward_kernel, grid=(GROUPS,), in_specs=[pl.BlockS...  31.1 us
    dot_general x3, matrix products, product(): return jnp.dot(left_side, right_side, preferred_element_type=jnp.float32)  25.5 us
    dot_general x3, matrix products, contract_cols(): lax.dot_general(left_side, right_side, NT, preferred_element_type=jnp.flo...  24.8 us
    dot_general x3, matrix products, contract_rows(): lax.dot_general(left_side, right_side, (((0,), (0,)), ((), ())), preferre...  23.2 us
    dot_general x2, matrix products, body(): lax.dot_general(jnp.broadcast_to(rows_in[None], (n_mp, *rows_in.shape)),...  16.6 us
  transfers between devices with their start and end apart: 4, of which 0 were waited for; matrix products, arithmetic and copies ran while one was open for 32% of the time, Pallas kernels for 44%

profile of v1, /device:TPU:0, one launch (start us, length us, event | category | flops | bytes accessed | tf_op | source)
XLA Modules:
  0.0 522.9 jit_solution(7485970384517161832)
XLA Ops:
  8.7 87.8 %shard_map.313 = (bf16[2,2,4,2,96,576]{5,4,3,2,1,0:T(8,128)(2,1)}, bf16[2,2,4,2,24,768]{5,4,3,2,1,0:T(8,128)(2,1)}, bf16[2,2,4,2,96,768]{5,4,3,2,1,0:T(8,128)(2,...) custom-call(bf16[96,576]{1,0:T(8,128)(2,1)} %pad_maximum_fusion.2.refs_0_, bf16[24,768]{1,0:T(8,128)(2,1)} %refs_1_.1, ...), custom_call_target="tpu_custom_call" | custom-call | tf_op jit(solution)/shard_map/pallas_call | solution.py:304
  102.6 11.6 %copy.114 = bf16[2,2,4,2,96,576]{4,3,2,5,1,0:T(2,128)(2,1)} copy(bf16[2,2,4,2,96,576]{5,4,3,2,1,0:T(8,128)(2,1)} %get-tuple-element.44) | data formatting | bytes 7077888 | tf_op jit(solution)/shard_map/pallas_call | solution.py:304
  114.2 13.0 %reshape_reshape.24 = bf16[4,768,3,192]{1,3,2,0:T(8,128)(2,1)S(1)} reshape(bf16[2,2,4,2,96,576]{4,3,2,5,1,0:T(2,128)(2,1)} %copy.114) | data formatting | bytes 7077888 | tf_op jit(solution)/shard_map/reshape;reshape | solution.py:497
  128.5 6.7 %copy.118 = bf16[4,768,768]{1,2,0:T(8,128)(2,1)} copy(bf16[4,768,768]{2,1,0:T(8,128)(2,1)} %bitcast.106) | data formatting | bytes 9437184 | tf_op jit(solution)/shard_map/reshape;reshape | solution.py:501
  137.7 2.6 pad.24
  148.2 9.8 %add_convert_fusion.qkv_ref = bf16[4,1024,768]{2,1,0:T(8,128)(2,1)} fusion(f32[4,768]{1,0:T(4,128)S(1)} %select_maximum_fusion, bf16[4,768,768]{1,2,0:T(8,128)(2,1)} %bitcast.98, bf16[1024,768]{0,1:T(8,128)(2,1)S(1)} %pad_maximum_fusion), kind=kOutput, calls=%fused_computation.8 | convolution fusion | flops 4838129664 | bytes 12595200 | tf_op jit(solution)/shard_map/dot_general | solution.py:510
  158.0 31.1 %shard_map.314 = (bf16[4,1024,256]{2,1,0:T(8,128)(2,1)}, f32[4,8,1024]{2,1,0:T(8,128)}) custom-call(bf16[1024,1]{1,0:T(8,128)(2,1)} %copy.113.bias_ref, bf16[4,1024,768]{2,1,0:T(8,128)(2,1)} %add_convert_fusion.qkv_ref), custom_call_target="tpu_custom_call" | custom-call | flops 15000000512 | bytes 10000000 | tf_op jit(solution)/shard_map/pallas_call | solution.py:91
  189.1 3.8 fusion.45
  193.6 10.7 %multiply_convert_fusion = (bf16[1024,3072]{1,0:T(8,128)(2,1)}, f32[1024,3072]{1,0:T(8,128)}) fusion(f32[3072]{0:T(1024)S(1)} %copy-done.19, bf16[768,3072]{0,1:T(8,128)(2,1)S(1)} %bitcast.102, f32[1024,768]{0,1:T(8,128)S(1)} %get-tuple-element.150, f32[768]{0:T(1024)S(1)} %copy-done.28, f32[768]{0:T(1024)S(1)} %copy-done.21, f32[1024]{0:T(1024)S(1)} %add_rsqrt_fusion.1, ...), kind=kOutput, calls=%fused_computation.6 | convolution fusion | flops 4854644736 | bytes 26765312 | tf_op jit(solution)/shard_map/dot_general | solution.py:28
  204.3 11.0 %fusion.13 = (f32[]{:T(128)}, f32[]{:T(128)}, f32[1024]{0:T(1024)S(1)}, f32[1024,768]{0,1:T(8,128)S(1)}) fusion(f32[1024,768,1]{0,1,2:T(8,128)S(1)} %get-tuple-element.179, f32[1024]{0:T(1024)S(1)} %fusion.33, f32[768]{0:T(1024)S(1)} %copy-done.26, f32[768]{0:T(1024)S(1)} %copy-done.27, f32[768]{0:T(1024)S(1)} %copy-done.28, f32[768]{0:T(1024)S(1)} %copy-done.21, ...), kind=kOutput, calls=%fused_computation.25 | convolution fusion | flops 4842847232 | bytes 20475912 | tf_op jit(solution)/shard_map/dot_general | solution.py:28
  216.5 3.8 fusion.11
  220.3 2.9 fusion.41
  223.2 10.0 %convolution_convert_fusion.1 = bf16[3072,768]{1,0:T(8,128)(2,1)} fusion(bf16[1024,3072]{1,0:T(8,128)(2,1)} %get-tuple-element.180, f32[1024,768]{0,1:T(8,128)S(1)} %get-tuple-element.144), kind=kOutput, calls=%fused_computation.10 | convolution fusion | flops 4834983936 | bytes 14155776 | tf_op jit(solution)/shard_map/dot_general | solution.py:32
  233.2 13.3 %fusion.51 = (f32[3072]{0:T(1024)S(1)}, bf16[1024,3072]{1,0:T(8,128)(2,1)}) fusion(f32[1024,3072]{1,0:T(8,128)} %get-tuple-element.181, f32[3072]{0:T(1024)S(1)} %copy-done.19, bf16[3072,768]{1,0:T(8,128)(2,1)S(1)} %bitcast.135, f32[1024,768]{0,1:T(8,128)S(1)} %get-tuple-element.144), kind=kOutput, calls=%fused_computation.111 | convolution fusion | flops 4870370304 | bytes 26763264 | tf_op jit(solution)/shard_map/dot_general | solution.py:38
  246.6 8.3 %multiply_reduce_fusion = (f32[768]{0:T(1024)S(1)}, f32[1024]{0:T(1024)S(1)}, f32[1024]{0:T(1024)S(1)}, f32[768]{0:T(1024)S(1)}, f32[1024,768]{0,1:T(8,128)S(1)}) fusion(f32[1024,768]{0,1:T(8,128)S(1)} %get-tuple-element.150, f32[1024]{0:T(1024)S(1)} %add_rsqrt_fusion.1, f32[1024]{0:T(1024)S(1)} %broadcast_multiply_fusion.5, f32[768]{0:T(1024)S(1)} %copy-done.21, ...), kind=kOutput, calls=%fused_computation.30 | convolution fusion | flops 4839698432 | bytes 20472832 | tf_op jit(solution)/shard_map/dot_general | solution.py:38
  254.9 9.8 %convolution_convert_fusion = bf16[768,3072]{1,0:T(8,128)(2,1)} fusion(bf16[1024,3072]{1,0:T(8,128)(2,1)} %get-tuple-element.184, f32[1024,768]{0,1:T(8,128)S(1)} %get-tuple-element.150, f32[768]{0:T(1024)S(1)} %copy-done.28, f32[768]{0:T(1024)S(1)} %copy-done.21, f32[1024]{0:T(1024)S(1)} %add_rsqrt_fusion.1, f32[1024]{0:T(1024)S(1)} %broadcast_multiply_fusion.5), kind=kOutput, calls=%fused_computation.9 | convolution fusion | flops 4838129664 | bytes 14170112 | tf_op jit(solution)/shard_map/dot_general | solution.py:32
  266.1 3.1 convolution_convert_fusion.2
  269.2 4.0 copy.124
  273.2 36.5 %shard_map.315 = (bf16[4,1024,768]{2,1,0:T(8,128)(2,1)}, f32[4,8,256]{2,1,0:T(8,128)}) custom-call(bf16[1024,1]{1,0:T(8,128)(2,1)} %copy.113.bias_ref, bf16[4,1024,768]{2,1,0:T(8,128)(2,1)} %add_convert_fusion.qkv_ref, bf16[4,1024,256]{2,1,0:T(8,128)(2,1)} %get-tuple-element.46.out_ref, f32[4,8,1024]{2,1,0:T(8,128)} %get-tuple-element.50.lse_ref, ...), custom_call_target="tpu_custom_call" | custom-call | flops 30000001024 | bytes 20000000 | tf_op jit(solution)/shard_map/pallas_call | solution.py:159
  309.7 9.3 %bitcast_add_fusion = f32[1024,768]{0,1:T(8,128)S(1)} fusion(f32[1024,768]{0,1:T(8,128)} %copy-done.3, bf16[4,1024,768]{2,1,0:T(8,128)(2,1)} %get-tuple-element.51, bf16[4,768,768]{1,2,0:T(8,128)(2,1)} %bitcast.99), kind=kOutput, calls=%fused_computation.28 | convolution fusion | flops 4832624640 | bytes 17301504 | tf_op jit(solution)/shard_map/dot_general | solution.py:569
  319.0 6.9 %fusion.21 = bf16[4,768,768]{2,1,0:T(8,128)(2,1)} fusion(bf16[4,1024,768]{2,1,0:T(8,128)(2,1)S(1)} %copy-done.29, bf16[1024,768]{0,1:T(8,128)(2,1)S(1)} %copy-done.10), kind=kOutput, calls=%fused_computation.47 | convolution fusion | flops 4834197504 | bytes 12582912 | tf_op jit(solution)/shard_map/dot_general | solution.py:562
  329.6 9.7 %reshape.231 = bf16[8,96,4,768]{3,2,1,0:T(4,128)(2,1)} reshape(bf16[768,3072]{1,0:T(8,128)(2,1)} %convolution_convert_fusion) | data formatting | bytes 9437184 | tf_op jit(solution)/shard_map/reshape | solution.py:586
  339.4 5.4 %copy.127 = bf16[8,96,4,768]{3,1,0,2:T(8,128)(2,1)} copy(bf16[8,96,4,768]{3,2,1,0:T(4,128)(2,1)} %reshape.231) | data formatting | bytes 9437184 | tf_op jit(solution)/shard_map/reshape | solution.py:586
  344.8 4.1 copy.128
  348.9 3.4 convolution_convert_fusion.3
  353.4 6.7 %copy.129 = bf16[4,768,768]{1,2,0:T(8,128)(2,1)} copy(bf16[4,768,768]{2,1,0:T(8,128)(2,1)} %fusion.21) | data formatting | bytes 9437184 | tf_op jit(solution)/shard_map/convert_element_type | solution.py:577
  360.1 11.5 %reshape.235 = bf16[4,8,96,3,256]{2,1,4,3,0:T(8,128)(2,1)} reshape(bf16[4,768,768]{1,2,0:T(8,128)(2,1)} %copy.129) | data formatting | bytes 9437184 | tf_op jit(solution)/shard_map/reshape | solution.py:578
  371.7 4.8 slice.150
  376.5 11.4 %copy.138.refs_3_ = bf16[2,2,4,2,96,576]{5,4,3,2,1,0:T(8,128)(2,1)} copy(bf16[2,2,4,2,96,576]{4,3,2,5,1,0:T(2,128)(2,1)} %bitcast.95) | data formatting | bytes 7077888 | tf_op jit(solution)/shard_map/reshape;reshape | solution.py:445
  389.6 2.7 pad_maximum_fusion.3
  393.1 109.4 %shard_map.316 = (f32[96,768]{1,0:T(8,128)}, f32[96,768]{1,0:T(8,128)}, f32[24,768]{1,0:T(8,128)}, f32[96,576]{1,0:T(8,128)}, f32[8,128]{1,0:T(8,128)}) custom-call(bf16[2,2,4,2,96,768]{5,4,3,2,1,0:T(8,128)(2,1)} %bitcast.97, bf16[2,2,4,2,96,768]{5,4,3,2,1,0:T(8,128)(2,1)} %bitcast.94, bf16[2,2,4,2,24,768]{5,4,3,2,1,0:T(8,128)(2,1)} %bitcast.96, ...), custom_call_target="tpu_custom_call" | custom-call | tf_op jit(solution)/shard_map/pallas_call | solution.py:421
  513.4 3.6 maximum_select_fusion
  (159 shorter events, 51.3 us)
Async XLA Ops:
  4.0 141.7 %collective-permute-start = (bf16[512,768]{0,1:T(8,128)(2,1)}, bf16[512,768]{0,1:T(8,128)(2,1)}, u32[]{:S(2)}, u32[]{:S(2)}) collective-permute-start(bf16[512,768]{0,1:T(8,128)(2,1)} %get-tuple-element.163), channel_id=1, source_target_pairs={{0,1},{1,0},{2,3},{3,2},{4,5},{5,4},{6,7},{7,6},{8,9},{9,8},{10,11... | collective-permute-start | bytes 2359304 | tf_op jit(solution)/shard_map/ppermute | solution.py:190
  4.8 2.5 copy-start.22
  4.8 2.5 copy-start.23
  4.8 2.5 copy-start.24
  4.8 3.1 copy-start.13
  4.8 3.1 copy-start.14
  4.9 3.1 copy-start.15
  5.4 94.4 %copy-start.25 = (s32[2,2]{1,0:T(2,128)S(1)}, s32[2,2]{1,0:T(2,128)}, u32[]{:S(2)}) copy-start(s32[2,2]{1,0:T(2,128)} %param.22) | copy-start | bytes 52
  6.8 209.0 %collective-permute-start.2 = (bf16[512,768]{0,1:T(8,128)(2,1)}, bf16[512,768]{0,1:T(8,128)(2,1)}, u32[]{:S(2)}, u32[]{:S(2)}) collective-permute-start(bf16[512,768]{0,1:T(8,128)(2,1)} %get-tuple-element.157), channel_id=1, source_target_pairs={{0,1},{1,0},{2,3},{3,2},{4,5},{5,4},{6,7},{7,6},{8,9},{9,8},{10,11... | collective-permute-start | bytes 2359304 | tf_op jit(solution)/shard_map/ppermute | solution.py:190
  99.1 3.5 copy-start.16
  137.7 2.6 copy-start.2
  137.7 5.2 copy-start.17
  140.3 5.5 %copy-start.6 = (bf16[512,768]{0,1:T(8,128)(2,1)S(1)}, bf16[512,768]{0,1:T(8,128)(2,1)}, u32[]{:S(2)}) copy-start(bf16[512,768]{0,1:T(8,128)(2,1)} %get-tuple-element.162) | copy-start | bytes 2359300
  158.0 31.1 %copy-start.1 = (bf16[4,192,768]{1,2,0:T(8,128)(2,1)S(1)}, bf16[4,192,768]{1,2,0:T(8,128)(2,1)}, u32[]{:S(2)}) copy-start(bf16[4,192,768]{1,2,0:T(8,128)(2,1)} %copy.117) | copy-start | bytes 3538948
  158.0 31.1 %copy-start.26 = (f32[768]{0:T(1024)S(1)}, f32[768]{0:T(1024)}, u32[]{:S(2)}) copy-start(f32[768]{0:T(1024)} %param.32) | copy-start | bytes 9220
  189.1 4.3 slice-start
  189.1 4.2 slice-start.1
  193.6 10.7 %copy-start.27 = (f32[768]{0:T(1024)S(1)}, f32[768]{0:T(1024)}, u32[]{:S(2)}) copy-start(f32[768]{0:T(1024)} %param.33) | copy-start | bytes 9220
  215.8 4.5 copy-start.20
  220.3 12.9 %slice-start.4 = ((s8[4718592]{0:T(1024)(128)(4,1)}), s8[4194304]{0:T(1024)(128)(4,1)S(1)}, s32[]{:S(2)}) async-start(s8[4718592]{0:T(1024)(128)(4,1)} %bitcast.133), calls=%async_computation.4 | async-start | bytes 8388608
  223.2 10.0 %slice-start.5 = ((s8[4718592]{0:T(1024)(128)(4,1)}), s8[524288]{0:T(1024)(128)(4,1)S(1)}, s32[]{:S(2)}) async-start(s8[4718592]{0:T(1024)(128)(4,1)} %bitcast.133), calls=%async_computation.5 | async-start | bytes 1048576
  223.2 23.4 %slice-start.2 = ((s8[4718592]{0:T(1024)(128)(4,1)}), s8[4194304]{0:T(1024)(128)(4,1)S(1)}, s32[]{:S(2)}) async-start(s8[4718592]{0:T(1024)(128)(4,1)} %bitcast.103), calls=%async_computation.2 | async-start | bytes 8388608
  233.2 13.3 %slice-start.3 = ((s8[4718592]{0:T(1024)(128)(4,1)}), s8[524288]{0:T(1024)(128)(4,1)S(1)}, s32[]{:S(2)}) async-start(s8[4718592]{0:T(1024)(128)(4,1)} %bitcast.103), calls=%async_computation.3 | async-start | bytes 1048576
  265.8 3.4 copy-start.3
  309.7 9.3 %copy-start.10 = (bf16[1024,768]{0,1:T(8,128)(2,1)S(1)}, bf16[1024,768]{0,1:T(8,128)(2,1)}, u32[]{:S(2)}) copy-start(bf16[1024,768]{0,1:T(8,128)(2,1)} %copy-done.9) | copy-start | bytes 4718596
  309.7 9.3 %copy-start.29 = (bf16[4,1024,768]{2,1,0:T(8,128)(2,1)S(1)}, bf16[4,1024,768]{2,1,0:T(8,128)(2,1)}, u32[]{:S(2)}) copy-start(bf16[4,1024,768]{2,1,0:T(8,128)(2,1)} %get-tuple-element.51) | copy-start | bytes 18874372
  327.2 183.1 %collective-permute-start.1 = (bf16[512,768]{0,1:T(8,128)(2,1)}, bf16[512,768]{0,1:T(8,128)(2,1)}, u32[]{:S(2)}, u32[]{:S(2)}) collective-permute-start(bf16[512,768]{0,1:T(8,128)(2,1)} %get-tuple-element.161), channel_id=1, source_target_pairs={{0,1},{1,0},{2,3},{3,2},{4,5},{5,4},{6,7},{7,6},{8,9},{9,8},{10,11... | collective-permute-start | bytes 2359304 | tf_op jit(solution)/shard_map/ppermute | solution.py:190
  329.5 184.0 %collective-permute-start.3 = (f32[512,768]{0,1:T(8,128)}, f32[512,768]{0,1:T(8,128)}, u32[]{:S(2)}, u32[]{:S(2)}) collective-permute-start(f32[512,768]{0,1:T(8,128)} %get-tuple-element.155), channel_id=1, source_target_pairs={{0,1},{1,0},{2,3},{3,2},{4,5},{5,4},{6,7},{7,6},{8,9},{9,8},{10,11... | collective-permute-start | bytes 4718600 | tf_op jit(solution)/shard_map/ppermute | solution.py:190
  344.8 4.2 copy-start.4
  393.1 117.2 %copy-start.5 = (bf16[1,512,768]{1,2,0:T(8,128)(2,1)S(1)}, bf16[1,512,768]{1,2,0:T(8,128)(2,1)}, u32[]{:S(2)}) copy-start(bf16[1,512,768]{1,2,0:T(8,128)(2,1)} %get-tuple-element.160) | copy-start | bytes 2359300
  517.1 2.4 copy-start.12
  517.1 4.7 copy-start.11
  (8 other events, 8.9 us)
